TPU v7x, 32 devices: a whole 2x2x4 slice. The times are simulated.
32 devices in a mesh: seq: 32 (over z, y, x, core).
Axes of the slice: x: 2, y: 2, z: 4, core: 2. Of those that a mesh axis runs over, the one named last changes fastest.
Arguments:
- tokens: bfloat16 [32768, 1024], P('seq'), may hold values from -16 to 16
- w_query: bfloat16 [1024, 1024], replicated, may hold values from -0.1875 to 0.1875
- w_key: bfloat16 [1024, 1024], replicated, may hold values from -0.1875 to 0.1875
- w_value: bfloat16 [1024, 1024], replicated, may hold values from -0.1875 to 0.1875
- w_out: bfloat16 [1024, 1024], replicated, may hold values from -0.1875 to 0.1875
- rand_blocks: int32 [512, 3], P('seq'), may hold values from 0 to 511, as said below
- global_pos: int32 [128], replicated, may hold values from 0 to 32767, as said below
Outputs:
- mixed: bfloat16 [32768, 1024], P('seq')
Inputs may be any that keep to these rules, and one draw needn't show every extreme that they name: `rand_blocks`: the entries of a row differ, and none is the row's block or a block next to it. All entries lie on the row's own device (blocks of 16 per device, contiguous), except that for each device and each offset o of -3 to -1 and 1 to 3 for which a device o away exists, exactly one row of the device has its last entry on the device o away. `global_pos`: distinct and increasing.
All inputs are finite; a program needn't handle non-finite values.
Results may differ from a plain program's by a relative error of at most 0.003.
The roundings to bfloat16 on the way count: a program that leaves them out, or rounds other values in their place, can miss the bound.
Values may be sent and summed in bfloat16 or wider, within the bound.
A program may use at most 192 MiB of HBM per device.

v0:
```python
import math

import jax
import jax.numpy as jnp
from jax import lax
from jax.sharding import PartitionSpec as P

HEADS = 16
HD = 64
BLK = 64
RAND = 3
NG = 128
FAR = 3


def padded_2(cells, sides, width):
    for axis, dim in sides:
        count = lax.axis_size(axis)
        ends = count - 1
        head = lax.slice_in_dim(cells, 0, width, axis=dim)
        tail = lax.slice_in_dim(cells, cells.shape[dim] - width, cells.shape[dim], axis=dim)
        cells = jnp.concatenate(
            [
                lax.ppermute(tail, axis, [(i, (i + 1) % count) for i in range(ends)]),
                cells,
                lax.ppermute(head, axis, [((i + 1) % count, i) for i in range(ends)]),
            ],
            axis=dim,
        )
    return cells


def passed_along(value, axis, steps):
    count = lax.axis_size(axis)
    initial, last = (max(0, -steps), min(count, count - steps))
    return lax.ppermute(value, axis, [(source, source + steps) for source in range(initial, last)])


def body(tokens, w_query, w_key, w_value, w_out, rand_blocks, global_pos):
    tok_dev = tokens.shape[0]
    model_width = tokens.shape[1]
    block_count = tok_dev // BLK
    seq_count = lax.axis_size("seq")
    device_index = lax.axis_index("seq")
    score_scale = 1.0 / math.sqrt(HD)
    queries = jnp.dot(tokens, w_query, preferred_element_type=jnp.float32).astype(jnp.bfloat16)
    keyval = jnp.concatenate(
        [
            jnp.dot(tokens, w_key, preferred_element_type=jnp.float32),
            jnp.dot(tokens, w_value, preferred_element_type=jnp.float32),
        ],
        axis=1,
    ).astype(jnp.bfloat16)
    padded = padded_2(keyval, (("seq", 0),), BLK)
    last_column = rand_blocks[:, RAND - 1]
    offset_list = list(range(-FAR, 0)) + list(range(1, FAR + 1))
    far_list = []
    for offset in offset_list:
        owner_dev = device_index + offset
        my_request = jnp.sum(
            jnp.where(
                last_column // block_count == owner_dev, last_column - owner_dev * block_count, 0
            )
        )
        wanted_block = passed_along(my_request, "seq", offset)
        wanted_block = jnp.clip(wanted_block, 0, block_count - 1)
        far_block = lax.dynamic_slice_in_dim(keyval, wanted_block * BLK, BLK, 0)
        far_list.append(passed_along(far_block, "seq", -offset))
    key_table = jnp.concatenate(
        [padded.reshape(block_count + 2, BLK, 2 * model_width), jnp.stack(far_list)], axis=0
    )
    owner_blocks = rand_blocks // block_count
    distance = owner_blocks - device_index
    slot_index = jnp.where(distance < 0, distance + FAR, distance + FAR - 1)
    random_index = jnp.where(
        distance == 0, rand_blocks - device_index * block_count + 1, block_count + 2 + slot_index
    )
    local_index = jnp.arange(block_count, dtype=jnp.int32)
    window_index = jnp.stack([local_index, local_index + 1, local_index + 2], axis=1)
    global_block = device_index * block_count + local_index
    window_ok = jnp.stack(
        [
            global_block > 0,
            jnp.ones((block_count,), bool),
            global_block < seq_count * block_count - 1,
        ],
        axis=1,
    )
    index_set = jnp.concatenate([window_index, random_index], axis=1)
    valid_set = jnp.concatenate([window_ok, jnp.ones((block_count, RAND), bool)], axis=1)
    owned = global_pos // tok_dev == device_index
    global_rows = jnp.clip(global_pos - device_index * tok_dev, 0, tok_dev - 1)
    own_part = jnp.where(owned[:, None], tokens[global_rows].astype(jnp.float32), 0.0)
    global_inputs = lax.psum(own_part, "seq").astype(jnp.bfloat16)
    global_queries = jnp.dot(global_inputs, w_query, preferred_element_type=jnp.float32).astype(
        jnp.bfloat16
    )
    global_keyval = jnp.concatenate(
        [
            jnp.dot(global_inputs, w_key, preferred_element_type=jnp.float32),
            jnp.dot(global_inputs, w_value, preferred_element_type=jnp.float32),
        ],
        axis=1,
    ).astype(jnp.bfloat16)
    global_keys = global_keyval[:, :model_width].reshape(NG, HEADS, HD)
    global_values = global_keyval[:, model_width:].reshape(NG, HEADS, HD)
    group_size = math.gcd(block_count, max(1, 512 // BLK))
    query_blocks = queries.reshape(block_count, BLK, HEADS, HD)

    def attend_group(start):
        chosen = lax.dynamic_slice_in_dim(index_set, start, group_size, 0)
        chosen_ok = lax.dynamic_slice_in_dim(valid_set, start, group_size, 0)
        key_rows = key_table[chosen].reshape(group_size, -1, 2 * model_width)
        key_heads = key_rows[..., :model_width].reshape(group_size, -1, HEADS, HD)
        value_heads = key_rows[..., model_width:].reshape(group_size, -1, HEADS, HD)
        key_valid = jnp.repeat(chosen_ok, BLK, axis=1)
        query_group = lax.dynamic_slice_in_dim(query_blocks, start, group_size, 0)
        local_scores = (
            jnp.einsum(
                "gqhd,gkhd->ghqk", query_group, key_heads, preferred_element_type=jnp.float32
            )
            * score_scale
        )
        local_scores = jnp.where(key_valid[:, None, None, :], local_scores, -1e30)
        global_scores = (
            jnp.einsum(
                "gqhd,khd->ghqk", query_group, global_keys, preferred_element_type=jnp.float32
            )
            * score_scale
        )
        all_scores = jnp.concatenate([local_scores, global_scores], axis=-1)
        top_score = jnp.max(all_scores, axis=-1, keepdims=True)
        exps = jnp.exp(all_scores - top_score)
        weights = (exps / jnp.sum(exps, axis=-1, keepdims=True)).astype(jnp.bfloat16)
        split_at = key_heads.shape[1]
        result = jnp.einsum(
            "ghqk,gkhd->gqhd",
            weights[..., :split_at],
            value_heads,
            preferred_element_type=jnp.float32,
        )
        result = result + jnp.einsum(
            "ghqk,khd->gqhd",
            weights[..., split_at:],
            global_values,
            preferred_element_type=jnp.float32,
        )
        return result.astype(jnp.bfloat16)

    starts = jnp.arange(0, block_count, group_size, dtype=jnp.int32)
    sparse = lax.map(attend_group, starts).reshape(tok_dev, model_width)
    local_keys = keyval[:, :model_width].reshape(tok_dev, HEADS, HD)
    local_values = keyval[:, model_width:].reshape(tok_dev, HEADS, HD)
    gscore = (
        jnp.einsum(
            "qhd,khd->hqk",
            global_queries.reshape(NG, HEADS, HD),
            local_keys,
            preferred_element_type=jnp.float32,
        )
        * score_scale
    )
    local_peak = jnp.max(gscore, axis=-1)
    gexp = jnp.exp(gscore - local_peak[:, :, None])
    stotal = jnp.sum(gexp, axis=-1)
    snum = jnp.einsum(
        "hqk,khd->qhd", gexp.astype(jnp.bfloat16), local_values, preferred_element_type=jnp.float32
    )
    peak_score = lax.pmax(local_peak, "seq")
    factor = jnp.exp(local_peak - peak_score)
    gtotal, gnum = lax.psum((stotal * factor, snum * jnp.transpose(factor)[:, :, None]), "seq")
    gout = (gnum / jnp.transpose(gtotal)[:, :, None]).reshape(NG, model_width).astype(jnp.bfloat16)
    target = jnp.where(owned, global_rows, tok_dev)
    attended = sparse.at[target].set(gout, mode="drop")
    return jnp.dot(attended, w_out, preferred_element_type=jnp.float32).astype(jnp.bfloat16)


def solution(mesh):
    placed = (P("seq", None), P(), P(), P(), P(), P("seq", None), P())
    return jax.shard_map(
        body, mesh=mesh, in_specs=placed, out_specs=P("seq", None), check_vma=False
    )
```

profile of v0, /device:TPU:0, one launch (start us, length us, event | category | flops | bytes accessed | tf_op | source)
XLA Modules:
  0.0 482.9 jit_solution(10202666505872828683)
XLA Ops:
  9.1 47.3 %all-reduce.4 = bf16[128,1024]{1,0:T(8,128)(2,1)S(1)} all-reduce(f32[128,1024]{1,0:T(8,128)S(1)} %convert_select_fusion), channel_id=1, replica_groups=mesh['seq'=32] {'seq'}, use_global_device_ids=true, to_apply=%region_6.7 | all-reduce | flops 131072 | bytes 786432 | tf_op jit(solution)/shard_map/psum | solution.py:94
  67.1 38.7 %pmax.7 = f32[16,128]{1,0:T(8,128)S(1)} all-reduce(f32[16,128]{1,0:T(8,128)S(1)} %get-tuple-element.113), channel_id=1, replica_groups=mesh['seq'=32] {'seq'}, use_global_device_ids=true, to_apply=%region_13.14 | all-reduce | flops 2048 | bytes 16384 | tf_op jit(solution)/shard_map/pmax | solution.py:169
  121.4 6.6 %collective-permute-start.12 = (s32[]{:T(128)}, s32[]{:T(128)}, u32[]{:S(2)}, u32[]{:S(2)}) collective-permute-start(s32[]{:T(128)} %get-tuple-element.71), channel_id=1, source_target_pairs={{0,3},{1,4},{2,5},{3,6},{4,7},{5,8},{6,9},{7,10},{8,11},{9,12},{10... | collective-permute-start | bytes 20 | tf_op jit(solution)/shard_map/ppermute | solution.py:36
  136.7 5.3 %convolution_convert_fusion.1 = bf16[1024,1024]{1,0:T(8,128)(2,1)} fusion(bf16[1024,1024]{1,0:T(8,128)(2,1)S(1)} %copy-done, bf16[1024,1024]{1,0:T(8,128)(2,1)} %param.10), kind=kOutput, calls=%fused_computation.50 | convolution fusion | flops 2148532224 | bytes 6291456 | tf_op jit(solution)/shard_map/dot_general | solution.py:46
  142.2 5.9 %collective-permute-start.10 = (s32[]{:T(128)}, s32[]{:T(128)}, u32[]{:S(2)}, u32[]{:S(2)}) collective-permute-start(s32[]{:T(128)} %get-tuple-element.72), channel_id=1, source_target_pairs={{0,2},{1,3},{2,4},{3,5},{4,6},{5,7},{6,8},{7,9},{8,10},{9,11},{10,... | collective-permute-start | bytes 20 | tf_op jit(solution)/shard_map/ppermute | solution.py:36
  166.0 6.3 %collective-permute-start.5 = (bf16[64,2048]{0,1:T(8,128)(2,1)}, bf16[64,2048]{0,1:T(8,128)(2,1)}, u32[]{:S(2)}, u32[]{:S(2)}) collective-permute-start(bf16[64,2048]{0,1:T(8,128)(2,1)} %get-tuple-element.107), channel_id=1, source_target_pairs={{0,2},{1,3},{2,4},{3,5},{4,6},{5,7},{6,8},{7,9},{8,10},{9,11},{10,... | collective-permute-start | bytes 786440 | tf_op jit(solution)/shard_map/ppermute | solution.py:36
  179.6 6.4 %reshape.76 = bf16[16,64,16,64]{3,2,1,0:T(8,128)(2,1)} reshape(bf16[1024,1024]{1,0:T(8,128)(2,1)} %convolution_convert_fusion.1) | data formatting | bytes 4194304 | tf_op jit(solution)/shard_map/reshape | solution.py:108
  186.0 60.5 %psum.23 = f32[128,16]{0,1:T(8,128)S(1)} all-reduce(f32[128,16]{0,1:T(8,128)S(1)} %get-tuple-element.110), channel_id=1, replica_groups=mesh['seq'=32] {'seq'}, use_global_device_ids=true, to_apply=%region_16.17 | all-reduce | flops 2048 | bytes 16384 | tf_op jit(solution)/shard_map/psum | solution.py:171
  246.5 24.6 %all-reduce.3.cloned.1.call-done = f32[128,16,64]{0,2,1:T(8,128)} async-done(((f32[128,16,64]{0,2,1:T(8,128)}), f32[128,16,64]{0,2,1:T(8,128)}) %all-reduce.3.cloned.1.call-update) | async-done | bytes 524304 | tf_op jit(solution)/shard_map/psum | solution.py:171
  273.0 9.4 %concatenate.23 = bf16[1152,2048]{0,1:T(8,128)(2,1)} concatenate(bf16[64,2048]{0,1:T(8,128)(2,1)} %collective-permute-done, bf16[1024,2048]{0,1:T(8,128)(2,1)} %pad_maximum_fusion, bf16[64,2048]{0,1:T(8,128)(2,1)} %collective-permute-done.1), dimensions={0} | concatenate | bytes 9437184 | tf_op jit(solution)/shard_map/concatenate | solution.py:22
  282.4 6.7 %copy.41 = bf16[1152,2048]{1,0:T(8,128)(2,1)} copy(bf16[1152,2048]{0,1:T(8,128)(2,1)} %concatenate.23) | data formatting | bytes 9437184 | tf_op jit(solution)/shard_map/concatenate | solution.py:22
  305.3 153.7 %while.10 = (s32[]{:T(128)}, bf16[2,8,64,16,64]{4,3,2,1,0:T(8,128)(2,1)}, s32[2]{0:T(128)S(1)}, s32[16,6]{1,0:T(8,128)S(1)}, bf16[24,64,2048]{2,1,0:T(8,128)(2,1...) while((s32[]{:T(128)}, ...), condition=%wide.region_11.12_spmd, body=%wide.region_7.11_spmd.sunk | while | flops 1115669632 | bytes 207407056 | solution.py:151
  307.9 9.2 %gather_fusion = bf16[48,64,2048]{2,1,0:T(8,128)(2,1)} fusion(bf16[24,64,2048]{2,1,0:T(8,128)(2,1)} %get-tuple-element.214, s32[1024]{0:T(1024)S(1)} %pad_clamp_fusion.3), kind=kCustom, calls=%fused_computation.clone.1 | custom fusion | bytes 25166016 | tf_op jit(solution)/shard_map/while/body/eval_jaxpr/gather | solution.py:113
  317.1 10.7 %fusion.93 = (bf16[8,384,1024]{2,1,0:T(8,128)(2,1)}, bf16[8,384,1024]{2,1,0:T(8,128)(2,1)}) fusion(bf16[8,384,2048]{2,1,0:T(8,128)(2,1)} %bitcast.118), kind=kLoop, calls=%fused_computation.131.clone.1 | loop fusion | bytes 25165824 | tf_op jit(solution)/shard_map/while/body/eval_jaxpr/slice | solution.py:115
  327.8 8.7 %copy.78 = bf16[8,384,1024]{1,2,0:T(8,128)(2,1)} copy(bf16[8,384,1024]{2,1,0:T(8,128)(2,1)} %get-tuple-element.181) | data formatting | bytes 12582912 | tf_op jit(solution)/shard_map/while
  358.9 8.7 %copy.79 = bf16[8,384,1024]{1,2,0:T(8,128)(2,1)} copy(bf16[8,384,1024]{2,1,0:T(8,128)(2,1)} %get-tuple-element.185) | data formatting | bytes 12582912 | tf_op jit(solution)/shard_map/while
  367.6 8.1 %fusion.97 = bf16[1,8,64,16,64]{2,4,3,1,0:T(8,128)(2,1)S(1)} fusion(f32[16,8,64,64]{2,3,0,1:T(8,128)} %fusion.96, bf16[8,384,16,64]{1,3,2,0:T(8,128)(2,1)} %bitcast.120, bf16[8,16,64,512]{3,2,1,0:T(8,128)(2,1)} %copy-done.2), kind=kOutput, calls=%fused_computation.17.clone.1 | convolution fusion | flops 403701760 | bytes 17825792 | tf_op jit(solution)/shard_map/while/body/eval_jaxpr/ghqk,gkhd->gqhd/dot_general | solution.py:136
  384.8 9.2 %gather_fusion = bf16[48,64,2048]{2,1,0:T(8,128)(2,1)} fusion(bf16[24,64,2048]{2,1,0:T(8,128)(2,1)} %get-tuple-element.214, s32[1024]{0:T(1024)S(1)} %pad_clamp_fusion.3), kind=kCustom, calls=%fused_computation.clone.1 | custom fusion | bytes 25166016 | tf_op jit(solution)/shard_map/while/body/eval_jaxpr/gather | solution.py:113
  394.0 10.7 %fusion.93 = (bf16[8,384,1024]{2,1,0:T(8,128)(2,1)}, bf16[8,384,1024]{2,1,0:T(8,128)(2,1)}) fusion(bf16[8,384,2048]{2,1,0:T(8,128)(2,1)} %bitcast.118), kind=kLoop, calls=%fused_computation.131.clone.1 | loop fusion | bytes 25165824 | tf_op jit(solution)/shard_map/while/body/eval_jaxpr/slice | solution.py:115
  404.7 8.7 %copy.78 = bf16[8,384,1024]{1,2,0:T(8,128)(2,1)} copy(bf16[8,384,1024]{2,1,0:T(8,128)(2,1)} %get-tuple-element.181) | data formatting | bytes 12582912 | tf_op jit(solution)/shard_map/while
  435.8 8.7 %copy.79 = bf16[8,384,1024]{1,2,0:T(8,128)(2,1)} copy(bf16[8,384,1024]{2,1,0:T(8,128)(2,1)} %get-tuple-element.185) | data formatting | bytes 12582912 | tf_op jit(solution)/shard_map/while
  444.5 8.1 %fusion.97 = bf16[1,8,64,16,64]{2,4,3,1,0:T(8,128)(2,1)S(1)} fusion(f32[16,8,64,64]{2,3,0,1:T(8,128)} %fusion.96, bf16[8,384,16,64]{1,3,2,0:T(8,128)(2,1)} %bitcast.120, bf16[8,16,64,512]{3,2,1,0:T(8,128)(2,1)} %copy-done.2), kind=kOutput, calls=%fused_computation.17.clone.1 | convolution fusion | flops 403701760 | bytes 17825792 | tf_op jit(solution)/shard_map/while/body/eval_jaxpr/ghqk,gkhd->gqhd/dot_general | solution.py:136
  459.0 6.5 %reshape.79 = bf16[1024,1024]{1,0:T(8,128)(2,1)} reshape(bf16[2,8,64,16,64]{4,3,2,1,0:T(8,128)(2,1)} %get-tuple-element.52) | data formatting | bytes 4194304 | tf_op jit(solution)/shard_map/reshape | solution.py:151
  470.1 5.9 %convolution_convert_fusion = bf16[1024,1024]{1,0:T(8,128)(2,1)} fusion(bf16[1024,1024]{1,0:T(8,128)(2,1)} %scatter_fusion, bf16[1024,1024]{1,0:T(8,128)(2,1)} %param.13), kind=kOutput, calls=%fused_computation.49 | convolution fusion | flops 2148532224 | bytes 6291456 | tf_op jit(solution)/shard_map/dot_general | solution.py:175
  (139 shorter events, 140.4 us)
Async XLA Ops:
  6.5 264.5 %all-reduce.3.cloned.1.call-start = ((), (), s32[]{:S(2)}) async-start(), calls=%async_computation | async-start | bytes 1048576 | tf_op jit(solution)/shard_map/psum | solution.py:171
  62.6 4.5 copy-start.3
  105.9 4.5 copy-start.7
  105.9 8.3 %slice-start = ((s8[8388608]{0:T(1024)(128)(4,1)}), s8[4194304]{0:T(1024)(128)(4,1)S(1)}, s32[]{:S(2)}) async-start(s8[8388608]{0:T(1024)(128)(4,1)} %bitcast.121), calls=%async_computation.1 | async-start | bytes 8388608
  118.3 24.0 %collective-permute-start.2 = (s32[]{:T(128)}, s32[]{:T(128)}, u32[]{:S(2)}, u32[]{:S(2)}) collective-permute-start(s32[]{:T(128)} %fusion.42), channel_id=1, source_target_pairs={{3,0},{4,1},{5,2},{6,3},{7,4},{8,5},{9,6},{10,7},{11,8},{12,9},{13... | collective-permute-start | bytes 20 | tf_op jit(solution)/shard_map/ppermute | solution.py:36
  119.6 29.3 %collective-permute-start.8 = (s32[]{:T(128)}, s32[]{:T(128)}, u32[]{:S(2)}, u32[]{:S(2)}) collective-permute-start(s32[]{:T(128)} %get-tuple-element.73), channel_id=1, source_target_pairs={{0,1},{1,2},{2,3},{3,4},{4,5},{5,6},{6,7},{7,8},{8,9},{9,10},{10,1... | collective-permute-start | bytes 20 | tf_op jit(solution)/shard_map/ppermute | solution.py:36
  121.4 28.0 %collective-permute-start.12 = (s32[]{:T(128)}, s32[]{:T(128)}, u32[]{:S(2)}, u32[]{:S(2)}) collective-permute-start(s32[]{:T(128)} %get-tuple-element.71), channel_id=1, source_target_pairs={{0,3},{1,4},{2,5},{3,6},{4,7},{5,8},{6,9},{7,10},{8,11},{9,12},{10... | collective-permute-start | bytes 20 | tf_op jit(solution)/shard_map/ppermute | solution.py:36
  128.0 22.1 %collective-permute-start.4 = (s32[]{:T(128)}, s32[]{:T(128)}, u32[]{:S(2)}, u32[]{:S(2)}) collective-permute-start(s32[]{:T(128)} %get-tuple-element.75), channel_id=1, source_target_pairs={{2,0},{3,1},{4,2},{5,3},{6,4},{7,5},{8,6},{9,7},{10,8},{11,9},{12,... | collective-permute-start | bytes 20 | tf_op jit(solution)/shard_map/ppermute | solution.py:36
  129.3 6.4 %copy-start.6 = (bf16[1024,1024]{1,0:T(8,128)(2,1)S(1)}, bf16[1024,1024]{1,0:T(8,128)(2,1)}, u32[]{:S(2)}) copy-start(bf16[1024,1024]{1,0:T(8,128)(2,1)} %param.11) | copy-start | bytes 6291460
  129.3 6.8 %copy-start.8 = (bf16[1024,1024]{1,0:T(8,128)(2,1)S(1)}, bf16[1024,1024]{1,0:T(8,128)(2,1)}, u32[]{:S(2)}) copy-start(bf16[1024,1024]{1,0:T(8,128)(2,1)} %param.12) | copy-start | bytes 6291460
  129.3 21.4 %collective-permute-start.6 = (s32[]{:T(128)}, s32[]{:T(128)}, u32[]{:S(2)}, u32[]{:S(2)}) collective-permute-start(s32[]{:T(128)} %get-tuple-element.74), channel_id=1, source_target_pairs={{1,0},{2,1},{3,2},{4,3},{5,4},{6,5},{7,6},{8,7},{9,8},{10,9},{11,1... | collective-permute-start | bytes 20 | tf_op jit(solution)/shard_map/ppermute | solution.py:36
  142.0 32.7 %copy-start.4 = (bf16[1024,1024]{0,1:T(8,128)(2,1)S(1)}, bf16[1024,1024]{0,1:T(8,128)(2,1)}, u32[]{:S(2)}) copy-start(bf16[1024,1024]{0,1:T(8,128)(2,1)} %copy-done.3) | copy-start | bytes 6291460
  142.2 18.1 %collective-permute-start.10 = (s32[]{:T(128)}, s32[]{:T(128)}, u32[]{:S(2)}, u32[]{:S(2)}) collective-permute-start(s32[]{:T(128)} %get-tuple-element.72), channel_id=1, source_target_pairs={{0,2},{1,3},{2,4},{3,5},{4,6},{5,7},{6,8},{7,9},{8,10},{9,11},{10,... | collective-permute-start | bytes 20 | tf_op jit(solution)/shard_map/ppermute | solution.py:36
  156.1 20.5 %collective-permute-start = (bf16[64,2048]{0,1:T(8,128)(2,1)}, bf16[64,2048]{0,1:T(8,128)(2,1)}, u32[]{:S(2)}, u32[]{:S(2)}) collective-permute-start(bf16[64,2048]{0,1:T(8,128)(2,1)} %get-tuple-element.104), channel_id=1, source_target_pairs={{0,1},{1,2},{2,3},{3,4},{4,5},{5,6},{6,7},{7,8},{8,9},{9,10},{10,1... | collective-permute-start | bytes 786440 | tf_op jit(solution)/shard_map/ppermute | solution.py:24
  159.0 19.0 %collective-permute-start.1 = (bf16[64,2048]{0,1:T(8,128)(2,1)}, bf16[64,2048]{0,1:T(8,128)(2,1)}, u32[]{:S(2)}, u32[]{:S(2)}) collective-permute-start(bf16[64,2048]{0,1:T(8,128)(2,1)} %get-tuple-element.105), channel_id=1, source_target_pairs={{1,0},{2,1},{3,2},{4,3},{5,4},{6,5},{7,6},{8,7},{9,8},{10,9},{11,1... | collective-permute-start | bytes 786440 | tf_op jit(solution)/shard_map/ppermute | solution.py:26
  161.0 128.1 %collective-permute-start.3 = (bf16[64,2048]{0,1:T(8,128)(2,1)}, bf16[64,2048]{0,1:T(8,128)(2,1)}, u32[]{:S(2)}, u32[]{:S(2)}) collective-permute-start(bf16[64,2048]{0,1:T(8,128)(2,1)} %get-tuple-element.106), channel_id=1, source_target_pairs={{0,3},{1,4},{2,5},{3,6},{4,7},{5,8},{6,9},{7,10},{8,11},{9,12},{10... | collective-permute-start | bytes 786440 | tf_op jit(solution)/shard_map/ppermute | solution.py:36
  166.0 125.6 %collective-permute-start.5 = (bf16[64,2048]{0,1:T(8,128)(2,1)}, bf16[64,2048]{0,1:T(8,128)(2,1)}, u32[]{:S(2)}, u32[]{:S(2)}) collective-permute-start(bf16[64,2048]{0,1:T(8,128)(2,1)} %get-tuple-element.107), channel_id=1, source_target_pairs={{0,2},{1,3},{2,4},{3,5},{4,6},{5,7},{6,8},{7,9},{8,10},{9,11},{10,... | collective-permute-start | bytes 786440 | tf_op jit(solution)/shard_map/ppermute | solution.py:36
  172.3 120.5 %collective-permute-start.7 = (bf16[64,2048]{0,1:T(8,128)(2,1)}, bf16[64,2048]{0,1:T(8,128)(2,1)}, u32[]{:S(2)}, u32[]{:S(2)}) collective-permute-start(bf16[64,2048]{0,1:T(8,128)(2,1)} %get-tuple-element.108), channel_id=1, source_target_pairs={{0,1},{1,2},{2,3},{3,4},{4,5},{5,6},{6,7},{7,8},{8,9},{9,10},{10,1... | collective-permute-start | bytes 786440 | tf_op jit(solution)/shard_map/ppermute | solution.py:36
  176.6 117.5 %collective-permute-start.9 = (bf16[64,2048]{0,1:T(8,128)(2,1)}, bf16[64,2048]{0,1:T(8,128)(2,1)S(1)}, u32[]{:S(2)}, u32[]{:S(2)}) collective-permute-start(bf16[64,2048]{0,1:T(8,128)(2,1)} %get-tuple-element.109), channel_id=1, source_target_pairs={{1,0},{2,1},{3,2},{4,3},{5,4},{6,5},{7,6},{8,7},{9,8},{10,9},{11,1... | collective-permute-start | bytes 786440 | tf_op jit(solution)/shard_map/ppermute | solution.py:36
  177.9 116.4 %collective-permute-start.11 = (bf16[64,2048]{0,1:T(8,128)(2,1)}, bf16[64,2048]{0,1:T(8,128)(2,1)S(1)}, u32[]{:S(2)}, u32[]{:S(2)}) collective-permute-start(bf16[64,2048]{0,1:T(8,128)(2,1)} %fusion.34), channel_id=1, source_target_pairs={{2,0},{3,1},{4,2},{5,3},{6,4},{7,5},{8,6},{9,7},{10,8},{11,9},{12,... | collective-permute-start | bytes 786440 | tf_op jit(solution)/shard_map/ppermute | solution.py:36
  289.1 10.7 %collective-permute-start.13 = (bf16[64,2048]{0,1:T(8,128)(2,1)S(1)}, bf16[64,2048]{0,1:T(8,128)(2,1)}, u32[]{:S(2)}, u32[]{:S(2)}) collective-permute-start(bf16[64,2048]{0,1:T(8,128)(2,1)S(1)} %get-tuple-element.103), channel_id=1, source_target_pairs={{3,0},{4,1},{5,2},{6,3},{7,4},{8,5},{9,6},{10,7},{11,8},{12,9},{13... | collective-permute-start | bytes 786440 | tf_op jit(solution)/shard_map/ppermute | solution.py:36
  459.0 6.5 %copy-start.9 = (bf16[128,1024]{1,0:T(8,128)(2,1)S(1)}, bf16[128,1024]{1,0:T(8,128)(2,1)}, u32[]{:S(2)}) copy-start(bf16[128,1024]{1,0:T(8,128)(2,1)} %copy.53) | copy-start | bytes 786436
  459.0 6.5 %copy-start.11 = (s32[128]{0:T(128)S(1)}, s32[128]{0:T(128)}, u32[]{:S(2)}) copy-start(s32[128]{0:T(128)} %get-tuple-element.94) | copy-start | bytes 1540
  465.6 10.4 %copy-start.1 = (bf16[1024,1024]{1,0:T(8,128)(2,1)S(1)}, bf16[1024,1024]{1,0:T(8,128)(2,1)}, u32[]{:S(2)}) copy-start(bf16[1024,1024]{1,0:T(8,128)(2,1)} %param.9) | copy-start | bytes 6291460
  (6 other events, 16.0 us)
Sparse Core Ops, SparseCore 0:
  117.0 154.0 all-reduce.2
where the time goes:
time: 481 us; the launch traced here: 483 us
  local copies, waits for them, and re-layouts  152 us (32%)
  blocking collectives  146 us (30%)
  matrix products  63.7 us (13%)
  starting transfers between devices  40.3 us (8%)
  other arithmetic  34.1 us (7%)
  waiting for transfers between devices  24.7 us (5%)
  between operations  17.7 us (4%)
    psum x1, blocking collectives, body(): lax.psum((stotal * factor, snum * jnp.transpose(factor)[:, :, None]), 'seq')  60.5 us
    psum x1, blocking collectives, body(): global_inputs = lax.psum(own_part, 'seq').astype(jnp.bfloat16)  47.3 us
    while x8, local copies, waits for them, and re-layouts  41.1 us
    pmax x1, blocking collectives, body(): peak_score = lax.pmax(local_peak, 'seq')  38.7 us
    ppermute x12, starting transfers between devices, passed_along(): lax.ppermute(value, axis, [(source, source + steps) for source in range(i...  36.2 us
    psum x1, waiting for transfers between devices, body(): lax.psum((stotal * factor, snum * jnp.transpose(factor)[:, :, None]), 'seq')  24.6 us
    slice x2, local copies, waits for them, and re-layouts, attend_group(): value_heads = key_rows[..., model_width:].reshape(group_size, -1, HEADS, HD)  21.5 us
    gather x2, local copies, waits for them, and re-layouts, attend_group(): key_rows = key_table[chosen].reshape(group_size, -1, 2 * model_width)  18.3 us
  transfers between devices with their start and end apart: 15, of which 1 were waited for; matrix products, arithmetic and copies ran while one was open for 11% of the time, Pallas kernels for 0%

commit v1 on v0

v1 whole, which is shorter than its diff:
```python
import functools
import math

import jax
import jax.numpy as jnp
from jax import lax
from jax.experimental import pallas as pl
from jax.experimental.pallas import tpu as pltpu
from jax.sharding import PartitionSpec as P

HEADS = 16
HD = 64
BLK = 64
RAND = 3
NG = 128
FAR = 3
OFFSETS = tuple(range(-FAR, 0)) + tuple(range(1, FAR + 1))
NFAR = len(OFFSETS)
GH = 4
GL = GH * HD
EXP_SCALE = math.log2(math.e) / math.sqrt(HD)
SCORE_SCALE = 1.0 / math.sqrt(HD)
MESH = pl.DeviceIdType.MESH
BF = jnp.bfloat16
F32 = jnp.float32


def mega(
    n,
    tok_hbm, wq_hbm, wk_hbm, wv_hbm, wo_hbm, req_ref, gcol_ref, grow_ref, idx_ref,
    out_ref,
    text, wq, wk, wv, wo, q, k, v, gq, sp, gf, sel, far,
    reqin, rs_out, rs_in, ag, cn_out, cn_in, cs_out, cs_in, ag2,
    load_sem, req_s, req_r, edge_s, edge_r,
    rs_s, rs_r, ag_s, ag_r, cn_s, cn_r, cs_s, cs_r, ag2_s, ag2_r,
):
    tok_dev, width = tok_hbm.shape
    nblk = tok_dev // BLK
    me = lax.axis_index("seq")
    _, rb, cb = ag.shape
    ncg = width // cb
    hpb = cb // HD
    groups = width // GL
    right0 = BLK + tok_dev
    far0 = right0 + BLK
    glob0 = far0 + NFAR * BLK

    own = text.at[pl.ds(BLK, tok_dev)]
    loads = [
        pltpu.make_async_copy(src, dst, load_sem.at[i])
        for i, (src, dst) in enumerate(
            ((tok_hbm, own), (wq_hbm, wq), (wk_hbm, wk), (wv_hbm, wv), (wo_hbm, wo))
        )
    ]
    for cp in loads:
        cp.start()

    text[0:BLK] = jnp.zeros((BLK, width), BF)
    text[right0:glob0] = jnp.zeros((glob0 - right0, width), BF)
    reqin[...] = jnp.zeros(reqin.shape, jnp.int32)

    barrier = pltpu.get_barrier_semaphore()

    def greet(o, c):
        pl.semaphore_signal(
            barrier, inc=1, device_id=(lax.rem(me + o, n),), device_id_type=MESH
        )
        return c

    lax.fori_loop(1, n, greet, 0)
    pl.semaphore_wait(barrier, n - 1)

    def to_all(src, dst, s_sem, r_sem):
        def one(o, c):
            peer = lax.rem(me + o, n)
            pltpu.make_async_remote_copy(
                src_ref=src(peer), dst_ref=dst.at[me], send_sem=s_sem, recv_sem=r_sem,
                device_id=(peer,), device_id_type=MESH,
            ).start()
            return c

        lax.fori_loop(1, n, one, 0)

    def wait_bytes(buf, sem):
        part = buf.at[pl.ds(0, n - 1)]
        pltpu.make_async_copy(part, part, sem).wait()

    def req_copy(i):
        return pltpu.make_async_remote_copy(
            src_ref=req_ref.at[i], dst_ref=reqin.at[i], send_sem=req_s.at[i],
            recv_sem=req_r.at[i], device_id=(me + OFFSETS[i],), device_id_type=MESH,
        )

    def far_copy(i):
        return pltpu.make_async_remote_copy(
            src_ref=far.at[pl.ds(i * BLK, BLK)],
            dst_ref=text.at[pl.ds(far0 + i * BLK, BLK)],
            send_sem=edge_s.at[2 + i], recv_sem=edge_r.at[2 + i],
            device_id=(me - OFFSETS[i],), device_id_type=MESH,
        )

    def halo_copy(side):
        if side == 0:
            src, dst, dev = (BLK, right0, me - 1)
        else:
            src, dst, dev = (right0 - BLK, 0, me + 1)
        return pltpu.make_async_remote_copy(
            src_ref=text.at[pl.ds(src, BLK)], dst_ref=text.at[pl.ds(dst, BLK)],
            send_sem=edge_s.at[side], recv_sem=edge_r.at[side],
            device_id=(dev,), device_id_type=MESH,
        )

    def exists(o):
        return me + o >= 0 if o < 0 else me + o < n

    for i, o in enumerate(OFFSETS):
        @pl.when(exists(o))
        def _():
            req_copy(i).start()

    loads[0].wait()
    for side, o in ((0, -1), (1, 1)):
        @pl.when(exists(o))
        def _():
            halo_copy(side).start()

    def project(src, s0, rows, w, dst, d0, step):
        def one(c, carry):
            a = pl.multiple_of(s0 + c * step, BLK)
            b = pl.multiple_of(d0 + c * step, BLK)
            val = jnp.dot(
                src[pl.ds(a, step)], w[...], preferred_element_type=F32
            ).astype(dst.dtype)
            if len(dst.shape) == 3:
                dst[pl.ds(d0 // BLK + c * (step // BLK), step // BLK)] = val.reshape(
                    step // BLK, BLK, width
                )
            else:
                dst[pl.ds(b, step)] = val
            return carry

        lax.fori_loop(0, rows // step, one, 0)

    hit = gcol_ref[...] == me * tok_dev + lax.broadcasted_iota(jnp.int32, (NG, tok_dev), 1)
    sel[0:NG] = jnp.where(hit, 1.0, 0.0).astype(BF)
    project(sel, 0, NG, own, gf, 0, NG)
    for d in range(n):
        r, c = (d // ncg) * rb, (d % ncg) * cb
        rs_out[d] = gf[r:r + rb, c:c + cb].astype(BF)
    to_all(lambda p: rs_out.at[p], rs_in, rs_s, rs_r)

    for i, o in enumerate(OFFSETS):
        @pl.when(exists(-o))
        def _():
            req_copy(i).wait_recv()
    col = lax.broadcasted_iota(jnp.int32, (BLK, tok_dev), 1)
    row = lax.broadcasted_iota(jnp.int32, (BLK, tok_dev), 0)
    for i in range(NFAR):
        want = reqin[i, 0:1, 0:1] * BLK
        sel[i * BLK:(i + 1) * BLK] = jnp.where(col == want + row, 1.0, 0.0).astype(BF)
    project(sel, 0, NFAR * BLK, own, far, 0, 2 * BLK)
    for i, o in enumerate(OFFSETS):
        @pl.when(exists(-o))
        def _():
            far_copy(i).start()

    loads[1].wait()
    project(text, BLK, tok_dev, wq, q, 0, 256)

    rs_in[me] = rs_out[me]
    wait_bytes(rs_in, rs_r)
    ag[me] = jnp.sum(rs_in[...].astype(F32), axis=0).astype(BF)
    to_all(lambda p: ag.at[me], ag, ag_s, ag_r)

    loads[2].wait()
    project(text, BLK, tok_dev, wk, k, BLK, 256)
    loads[3].wait()
    project(text, BLK, tok_dev, wv, v, BLK, 256)

    wait_bytes(ag, ag_r)
    for d in range(n):
        r, c = (d // ncg) * rb, (d % ncg) * cb
        gf[r:r + rb, c:c + cb] = ag[d].astype(F32)
    text[glob0:glob0 + NG] = gf[...].astype(BF)
    project(text, glob0, NG, wq, gq, 0, NG)

    lane = lax.broadcasted_iota(jnp.int32, (1, GL), 1) // HD
    masks = [jnp.where(lane == h, 1.0, 0.0).astype(BF) for h in range(GH)]
    lane_f = lax.broadcasted_iota(jnp.int32, (1, 128), 1)

    def stacked(x):
        return jnp.concatenate([x * m for m in masks], axis=0)

    def unstacked(x, rows):
        y = x[0:rows]
        for h in range(1, GH):
            y = jnp.where(lane == h, x[h * rows:(h + 1) * rows], y)
        return y

    NT = (((1,), (1,)), ((), ()))
    for g in range(groups):
        ls = slice(g * GL, (g + 1) * GL)
        s = lax.dot_general(
            stacked(gq[:, ls]), k[1:1 + nblk, :, ls].reshape(tok_dev, GL), NT, preferred_element_type=F32
        )
        m = jnp.max(s, axis=-1, keepdims=True)
        e = jnp.exp2((s - m) * EXP_SCALE)
        t = jnp.sum(e, axis=-1, keepdims=True)
        num = unstacked(
            jnp.dot(e.astype(BF), v[1:1 + nblk, :, ls].reshape(tok_dev, GL), preferred_element_type=F32), NG
        )
        m = m * SCORE_SCALE
        for part in range(GL // cb):
            stat = jnp.zeros((NG, 128), F32)
            for j in range(hpb):
                h = part * hpb + j
                stat = jnp.where(lane_f == j, m[h * NG:(h + 1) * NG], stat)
                stat = jnp.where(lane_f == hpb + j, t[h * NG:(h + 1) * NG], stat)
            cg = g * (GL // cb) + part
            for rg in range(NG // rb):
                d = rg * ncg + cg
                cn_out[d] = num[rg * rb:(rg + 1) * rb, part * cb:(part + 1) * cb].astype(BF)
                cs_out[d] = stat[rg * rb:(rg + 1) * rb]
    to_all(lambda p: cs_out.at[p], cs_in, cs_s, cs_r)
    to_all(lambda p: cn_out.at[p], cn_in, cn_s, cn_r)

    for side, o in ((0, 1), (1, -1)):
        @pl.when(exists(o))
        def _():
            halo_copy(side).wait_recv()
    for i, o in enumerate(OFFSETS):
        @pl.when(exists(o))
        def _():
            far_copy(i).wait_recv()
    for w, dst in ((wk, k), (wv, v)):
        project(text, 0, BLK, w, dst, 0, BLK)
        project(text, right0, glob0 + NG - right0, w, dst, right0, 192)

    keys_all = (3 + RAND) * BLK + NG
    key_col = lax.broadcasted_iota(jnp.int32, (1, keys_all), 1)

    def attend(b, carry):
        lead = jnp.where((me == 0) & (b == 0), BLK, 0)
        tail = jnp.where((me == n - 1) & (b == nblk - 1), 2 * BLK, 3 * BLK)
        bad = (key_col < lead) | ((key_col >= tail) & (key_col < 3 * BLK))
        bias = jnp.where(bad, -1e30, 0.0)
        at = pl.multiple_of(b * BLK, BLK)
        picks = [idx_ref[b * RAND + r] for r in range(RAND)]

        def rows(ref, ls):
            return jnp.concatenate(
                [ref[pl.ds(b, 3), :, ls].reshape(3 * BLK, GL)]
                + [ref[i, :, ls] for i in picks]
                + [ref[glob0 // BLK:, :, ls].reshape(NG, GL)],
                axis=0,
            )

        for g in range(groups):
            ls = slice(g * GL, (g + 1) * GL)
            s = lax.dot_general(
                stacked(q[pl.ds(at, BLK), ls]), rows(k, ls), NT, preferred_element_type=F32
            )
            s = s + bias
            m = jnp.max(s, axis=-1, keepdims=True)
            e = jnp.exp2((s - m) * EXP_SCALE)
            inv = 1.0 / jnp.sum(e, axis=-1, keepdims=True)
            o = jnp.dot((e * inv).astype(BF), rows(v, ls), preferred_element_type=F32)
            sp[pl.ds(at, BLK), ls] = unstacked(o, BLK).astype(BF)
        return carry

    lax.fori_loop(0, nblk // 2, attend, 0)

    cs_in[me] = cs_out[me]
    cn_in[me] = cn_out[me]
    wait_bytes(cs_in, cs_r)
    wait_bytes(cn_in, cn_r)
    peak = jnp.max(cs_in[...], axis=0)
    lane_c = lax.broadcasted_iota(jnp.int32, (1, cb), 1) // HD

    def spread(x, first):
        y = jnp.broadcast_to(x[:, first:first + 1], (rb, cb))
        for j in range(1, hpb):
            y = jnp.where(lane_c == j, x[:, first + j:first + j + 1], y)
        return y

    def merge(s, c):
        num, den = c
        stat = cs_in[s]
        fac = spread(jnp.exp(stat - peak), 0)
        return num + cn_in[s].astype(F32) * fac, den + spread(stat, hpb) * fac

    zero = jnp.zeros((rb, cb), F32)
    num, den = lax.fori_loop(0, n, merge, (zero, zero))
    ag2[me] = (num / den).astype(BF)
    to_all(lambda p: ag2.at[me], ag2, ag2_s, ag2_r)

    lax.fori_loop(nblk // 2, nblk, attend, 0)

    wait_bytes(ag2, ag2_r)
    for d in range(n):
        r, c = (d // ncg) * rb, (d % ncg) * cb
        gf[r:r + rb, c:c + cb] = ag2[d].astype(F32)
    gq[...] = gf[...].astype(BF)
    loads[4].wait()
    step = 256

    def finish(c, carry):
        at = pl.multiple_of(c * step, step)
        pos = me * tok_dev + at + lax.broadcasted_iota(jnp.int32, (step, NG), 0)
        one = jnp.where(pos == grow_ref[...], 1.0, 0.0)
        is_g = jnp.max(one, axis=-1, keepdims=True) > 0.5
        put = jnp.dot(one.astype(BF), gq[...], preferred_element_type=F32)
        att = jnp.where(is_g, put, sp[pl.ds(at, step)].astype(F32)).astype(BF)
        out_ref[pl.ds(at, step)] = jnp.dot(
            att, wo[...], preferred_element_type=F32
        ).astype(BF)
        return carry

    lax.fori_loop(0, tok_dev // step, finish, 0)

    for i, o in enumerate(OFFSETS):
        @pl.when(exists(o))
        def _():
            req_copy(i).wait_send()

        @pl.when(exists(-o))
        def _():
            far_copy(i).wait_send()
    for side, o in ((0, -1), (1, 1)):
        @pl.when(exists(o))
        def _():
            halo_copy(side).wait_send()
    for buf, sem in ((rs_out, rs_s), (ag, ag_s), (cn_out, cn_s), (cs_out, cs_s), (ag2, ag2_s)):
        wait_bytes(buf, sem)


def body(n, tokens, w_query, w_key, w_value, w_out, rand_blocks, global_pos):
    tok_dev, width = tokens.shape
    nblk = tok_dev // BLK
    me = lax.axis_index("seq")
    last = rand_blocks[:, RAND - 1]
    owner = last // nblk
    offs = jnp.array(OFFSETS, jnp.int32)
    mine = owner[None, :] == (me + offs)[:, None]
    want = jnp.sum(jnp.where(mine, (last - owner * nblk)[None, :], 0), axis=1)
    req = jnp.broadcast_to(want[:, None, None], (NFAR, 8, 128)).astype(jnp.int32)
    dist = rand_blocks // nblk - me
    slot = jnp.where(dist < 0, dist + FAR, dist + FAR - 1)
    idx = jnp.where(dist == 0, rand_blocks - me * nblk + 1, nblk + 2 + slot)
    idx = idx.reshape(-1).astype(jnp.int32)

    cb = 256 if n <= 32 else 128
    rb = NG * width // (n * cb)
    ext = tok_dev + 2 * BLK + NFAR * BLK + NG
    dma = pltpu.SemaphoreType.DMA
    vm = pltpu.VMEM
    blocks = vm((ext // BLK, BLK, width), BF)
    square = vm((width, width), BF)
    piece = vm((n, rb, cb), BF)
    stat = vm((n, rb, 128), F32)
    scratch = [
        vm((ext, width), BF), square, square, square, square,
        vm((tok_dev, width), BF), blocks, blocks,
        vm((NG, width), BF), vm((tok_dev, width), BF), vm((NG, width), F32),
        vm((NFAR * BLK, tok_dev), BF), vm((NFAR * BLK, width), BF),
        vm((NFAR, 8, 128), jnp.int32),
        piece, piece, piece, piece, piece, stat, stat, piece,
        dma((5,)), dma((NFAR,)), dma((NFAR,)), dma((2 + NFAR,)), dma((2 + NFAR,)),
    ] + [dma(())] * 10
    anyspace = pl.BlockSpec(memory_space=pl.ANY)
    vmem = pl.BlockSpec(memory_space=pltpu.VMEM)
    return pl.pallas_call(
        functools.partial(mega, n),
        out_shape=jax.ShapeDtypeStruct((tok_dev, width), BF),
        in_specs=[anyspace] * 5 + [vmem] * 3 + [pl.BlockSpec(memory_space=pltpu.SMEM)],
        out_specs=vmem,
        scratch_shapes=scratch,
        compiler_params=pltpu.CompilerParams(
            collective_id=0, has_side_effects=True, vmem_limit_bytes=60 << 20
        ),
        name="sublayer",
    )(
        tokens, w_query, w_key, w_value, w_out, req,
        global_pos.reshape(NG, 1), global_pos.reshape(1, NG), idx,
    )


def solution(mesh):
    placed = (P("seq", None), P(), P(), P(), P(), P("seq", None), P())
    return jax.shard_map(
        functools.partial(body, mesh.shape["seq"]), mesh=mesh, in_specs=placed,
        out_specs=P("seq", None), check_vma=False,
    )
```

time: 481 us -> 77.4 us (0.16)
  local copies, waits for them, and re-layouts: 152 us -> 5.83 us
  blocking collectives: 146 us -> 0 us
  Pallas kernels: 0 us -> 69.1 us
  matrix products: 63.7 us -> 0 us
  starting transfers between devices: 40.3 us -> 0 us
  other arithmetic: 34.1 us -> 2.23 us
  waiting for transfers between devices: 24.7 us -> 0 us
  between operations: 17.7 us -> 0.01 us
    psum x2 -> x0, blocking collectives: 108 us -> none  [the longest x1 60.5 us: body(): lax.psum((stotal * factor, snum * jnp.transpose(factor)[:, :, None]), 'seq')]
    pallas_call x0 -> x1, Pallas kernels: none -> 69.1 us  [body(): pl.pallas_call(functools.partial(mega, n), out_shape=jax.ShapeDtypeStruct...]
    dot_general x17 -> x0, matrix products: 63.7 us -> none  [the longest x2 16.2 us: attend_group(): jnp.einsum('ghqk,gkhd->gqhd', weights[..., :split_at], value_heads, prefe...]
    while x8 -> x0, local copies, waits for them, and re-layouts: 41.1 us -> none
    ppermute x14 -> x0, starting transfers between devices: 40.3 us -> none  [the longest x12 36.2 us: passed_along(): lax.ppermute(value, axis, [(source, source + steps) for source in range(i...]
    pmax x1 -> x0, blocking collectives: 38.7 us -> none  [body(): peak_score = lax.pmax(local_peak, 'seq')]
    psum x1 -> x0, waiting for transfers between devices: 24.6 us -> none  [body(): lax.psum((stotal * factor, snum * jnp.transpose(factor)[:, :, None]), 'seq')]
    slice x4 -> x0, local copies, waits for them, and re-layouts: 21.8 us -> none  [the longest x2 21.5 us: attend_group(): value_heads = key_rows[..., model_width:].reshape(group_size, -1, HEADS, HD)]
  transfers between devices with their start and end apart: 15 -> 0, of which waited for: 1 -> 0; matrix products, arithmetic and copies ran while one was open for 11% -> 0% of each run, Pallas kernels for 0% -> 0%
where the time goes in v1:
time: 77.4 us; the launch traced here: 77.1 us
  Pallas kernels  69.1 us (89%)
  local copies, waits for them, and re-layouts  5.83 us (8%)
  other arithmetic  2.23 us (3%)
    pallas_call x1, Pallas kernels, body(): pl.pallas_call(functools.partial(mega, n), out_shape=jax.ShapeDtypeStruct...  69.1 us
    unnamed x1, local copies, waits for them, and re-layouts  3.08 us

profile of v1, /device:TPU:0, one launch (start us, length us, event | category | flops | bytes accessed | tf_op | source)
XLA Modules:
  0.0 77.1 jit_solution(5076624988587301161)
XLA Ops:
  0.0 0.7 broadcast_add_fusion
  0.7 0.7 add_select_fusion.1
  1.4 0.7 bitcast_subtract_fusion
  2.0 0.2 select_reduce_fusion
  2.2 0.1 copy.13
  2.3 0.6 reshape.55.idx_ref
  2.9 0.7 broadcast_in_dim.23.req_ref
  3.6 1.4 %copy.14.gcol_ref = s32[128,1]{1,0:T(8,128)} copy(s32[128,1]{0,1:T(1,128)} %bitcast.12) | data formatting | bytes 1024 | tf_op jit(solution)/shard_map/reshape | solution.py:384
  5.0 69.1 %sublayer.1 = bf16[1024,1024]{1,0:T(8,128)(2,1)} custom-call(bf16[1024,1024]{1,0:T(8,128)(2,1)} %tok_hbm.1, bf16[1024,1024]{1,0:T(8,128)(2,1)} %wq_hbm.1, bf16[1024,1024]{1,0:T(8,128)(2,1)} %wk_hbm.1, bf16[1024,1024]{1,0:T(8,128)(2,1)} %wv_hbm.1, bf16[1024,1024]{1,0:T(8,128)(2,1)} %wo_hbm.1, s32[6,8,128]{2,1,0:T(8,128)} %broadcast_in_dim.23.req_ref, ...), custom_call_target="tpu_custom_call" | custom-call | tf_op jit(solution)/shard_map/sublayer/pallas_call | solution.py:372
  74.1 3.1 %copy.16 = bf16[1024,1024]{1,0:T(8,128)(2,1)} copy(bf16[1024,1024]{1,0:T(8,128)(2,1)} %sublayer.1) | data formatting | bytes 4194304

commit v2 on v1

--- a/solution.py
+++ b/solution.py
@@ -27,10 +27,10 @@
 
 def mega(
     n,
-    tok_hbm, wq_hbm, wk_hbm, wv_hbm, wo_hbm, req_ref, gcol_ref, grow_ref, idx_ref,
+    tok_hbm, wq_hbm, wk_hbm, wv_hbm, wo_hbm, rbv_ref, grow_ref, rb_ref,
     out_ref,
     text, wq, wk, wv, wo, q, k, v, gq, sp, gf, sel, far,
-    reqin, rs_out, rs_in, ag, cn_out, cn_in, cs_out, cs_in, ag2,
+    req_out, reqin, order, place, rs_out, rs_in, ag, cn_out, cn_in, cs_out, cs_in, ag2,
     load_sem, req_s, req_r, edge_s, edge_r,
     rs_s, rs_r, ag_s, ag_r, cn_s, cn_r, cs_s, cs_r, ag2_s, ag2_r,
 ):
@@ -57,7 +57,12 @@
 
     text[0:BLK] = jnp.zeros((BLK, width), BF)
     text[right0:glob0] = jnp.zeros((glob0 - right0, width), BF)
-    reqin[...] = jnp.zeros(reqin.shape, jnp.int32)
+    reqin[...] = jnp.zeros(reqin.shape, F32)
+    base = rbv_ref[:, RAND - 1:RAND] - me * nblk
+    for i, o in enumerate(OFFSETS):
+        loc = base - o * nblk
+        loc = jnp.where((loc >= 0) & (loc < nblk), loc, 0).astype(F32)
+        req_out[i] = jnp.broadcast_to(jnp.sum(loc, axis=0, keepdims=True), (8, 128))
 
     barrier = pltpu.get_barrier_semaphore()
 
@@ -87,7 +92,7 @@
 
     def req_copy(i):
         return pltpu.make_async_remote_copy(
-            src_ref=req_ref.at[i], dst_ref=reqin.at[i], send_sem=req_s.at[i],
+            src_ref=req_out.at[i], dst_ref=reqin.at[i], send_sem=req_s.at[i],
             recv_sem=req_r.at[i], device_id=(me + OFFSETS[i],), device_id_type=MESH,
         )
 
@@ -119,11 +124,6 @@
             req_copy(i).start()
 
     loads[0].wait()
-    for side, o in ((0, -1), (1, 1)):
-        @pl.when(exists(o))
-        def _():
-            halo_copy(side).start()
-
     def project(src, s0, rows, w, dst, d0, step):
         def one(c, carry):
             a = pl.multiple_of(s0 + c * step, BLK)
@@ -141,7 +141,13 @@
 
         lax.fori_loop(0, rows // step, one, 0)
 
-    hit = gcol_ref[...] == me * tok_dev + lax.broadcasted_iota(jnp.int32, (NG, tok_dev), 1)
+    diag = lax.broadcasted_iota(jnp.int32, (NG, NG), 0) == lax.broadcasted_iota(
+        jnp.int32, (NG, NG), 1
+    )
+    gcol = jnp.sum(
+        jnp.where(diag, (grow_ref[...] - me * tok_dev).astype(F32), 0.0), axis=1, keepdims=True
+    )
+    hit = gcol == lax.broadcasted_iota(jnp.int32, (NG, tok_dev), 1).astype(F32)
     sel[0:NG] = jnp.where(hit, 1.0, 0.0).astype(BF)
     project(sel, 0, NG, own, gf, 0, NG)
     for d in range(n):
@@ -149,20 +155,34 @@
         rs_out[d] = gf[r:r + rb, c:c + cb].astype(BF)
     to_all(lambda p: rs_out.at[p], rs_in, rs_s, rs_r)
 
+    lates = []
+    for b in range(nblk):
+        if b in (0, nblk - 1):
+            lates.append(jnp.int32(1))
+        else:
+            r = rb_ref[b, RAND - 1] - me * nblk
+            lates.append(jnp.where((r >= 0) & (r < nblk), 0, 1))
+    early = nblk - sum(lates)
+    seen = jnp.int32(0)
+    spots = []
+    for b in range(nblk):
+        spots.append(jnp.where(lates[b] == 1, early + seen, b - seen))
+        seen = seen + lates[b]
+        place[b] = spots[b]
+    for t in range(nblk):
+        order[t] = sum(jnp.where(spots[b] == t, b, 0) for b in range(nblk))
+
     for i, o in enumerate(OFFSETS):
         @pl.when(exists(-o))
         def _():
             req_copy(i).wait_recv()
     col = lax.broadcasted_iota(jnp.int32, (BLK, tok_dev), 1)
     row = lax.broadcasted_iota(jnp.int32, (BLK, tok_dev), 0)
+    away = (col - row).astype(F32)
     for i in range(NFAR):
         want = reqin[i, 0:1, 0:1] * BLK
-        sel[i * BLK:(i + 1) * BLK] = jnp.where(col == want + row, 1.0, 0.0).astype(BF)
+        sel[i * BLK:(i + 1) * BLK] = jnp.where(away == want, 1.0, 0.0).astype(BF)
     project(sel, 0, NFAR * BLK, own, far, 0, 2 * BLK)
-    for i, o in enumerate(OFFSETS):
-        @pl.when(exists(-o))
-        def _():
-            far_copy(i).start()
 
     loads[1].wait()
     project(text, BLK, tok_dev, wq, q, 0, 256)
@@ -171,6 +191,14 @@
     wait_bytes(rs_in, rs_r)
     ag[me] = jnp.sum(rs_in[...].astype(F32), axis=0).astype(BF)
     to_all(lambda p: ag.at[me], ag, ag_s, ag_r)
+    for side, o in ((0, -1), (1, 1)):
+        @pl.when(exists(o))
+        def _():
+            halo_copy(side).start()
+    for i, o in enumerate(OFFSETS):
+        @pl.when(exists(-o))
+        def _():
+            far_copy(i).start()
 
     loads[2].wait()
     project(text, BLK, tok_dev, wk, k, BLK, 256)
@@ -224,32 +252,30 @@
     to_all(lambda p: cs_out.at[p], cs_in, cs_s, cs_r)
     to_all(lambda p: cn_out.at[p], cn_in, cn_s, cn_r)
 
-    for side, o in ((0, 1), (1, -1)):
-        @pl.when(exists(o))
-        def _():
-            halo_copy(side).wait_recv()
-    for i, o in enumerate(OFFSETS):
-        @pl.when(exists(o))
-        def _():
-            far_copy(i).wait_recv()
     for w, dst in ((wk, k), (wv, v)):
-        project(text, 0, BLK, w, dst, 0, BLK)
-        project(text, right0, glob0 + NG - right0, w, dst, right0, 192)
+        project(text, glob0, NG, w, dst, glob0, NG)
 
     keys_all = (3 + RAND) * BLK + NG
     key_col = lax.broadcasted_iota(jnp.int32, (1, keys_all), 1)
 
-    def attend(b, carry):
-        lead = jnp.where((me == 0) & (b == 0), BLK, 0)
-        tail = jnp.where((me == n - 1) & (b == nblk - 1), 2 * BLK, 3 * BLK)
-        bad = (key_col < lead) | ((key_col >= tail) & (key_col < 3 * BLK))
-        bias = jnp.where(bad, -1e30, 0.0)
-        at = pl.multiple_of(b * BLK, BLK)
-        picks = [idx_ref[b * RAND + r] for r in range(RAND)]
+    def attend(late, t, carry):
+        b = order[t]
+        picks = []
+        for r in range(RAND):
+            rel = rb_ref[b, r] - me * nblk
+            dev = lax.div(rel + FAR * nblk, nblk)
+            slot = jnp.where(dev < FAR, dev, dev - 1)
+            pick = jnp.where(dev == FAR, rel + 1, nblk + 2 + slot)
+            picks.append(jnp.minimum(jnp.maximum(pick, 0), nblk + 1 + NFAR))
+        if late:
+            lead = jnp.where((me == 0) & (b == 0), BLK, 0)
+            tail = jnp.where((me == n - 1) & (b == nblk - 1), 2 * BLK, 3 * BLK)
+            bad = (key_col < lead) | ((key_col >= tail) & (key_col < 3 * BLK))
+            bias = jnp.where(bad, -1e30, 0.0)
 
         def rows(ref, ls):
             return jnp.concatenate(
-                [ref[pl.ds(b, 3), :, ls].reshape(3 * BLK, GL)]
+                [ref[b + i, :, ls] for i in range(3)]
                 + [ref[i, :, ls] for i in picks]
                 + [ref[glob0 // BLK:, :, ls].reshape(NG, GL)],
                 axis=0,
@@ -258,17 +284,18 @@
         for g in range(groups):
             ls = slice(g * GL, (g + 1) * GL)
             s = lax.dot_general(
-                stacked(q[pl.ds(at, BLK), ls]), rows(k, ls), NT, preferred_element_type=F32
+                stacked(q[b, :, ls]), rows(k, ls), NT, preferred_element_type=F32
             )
-            s = s + bias
+            if late:
+                s = s + bias
             m = jnp.max(s, axis=-1, keepdims=True)
             e = jnp.exp2((s - m) * EXP_SCALE)
             inv = 1.0 / jnp.sum(e, axis=-1, keepdims=True)
             o = jnp.dot((e * inv).astype(BF), rows(v, ls), preferred_element_type=F32)
-            sp[pl.ds(at, BLK), ls] = unstacked(o, BLK).astype(BF)
+            sp[t, :, ls] = unstacked(o, BLK).astype(BF)
         return carry
 
-    lax.fori_loop(0, nblk // 2, attend, 0)
+    lax.fori_loop(0, nblk // 2, functools.partial(attend, False), 0)
 
     cs_in[me] = cs_out[me]
     cn_in[me] = cn_out[me]
@@ -294,7 +321,20 @@
     ag2[me] = (num / den).astype(BF)
     to_all(lambda p: ag2.at[me], ag2, ag2_s, ag2_r)
 
-    lax.fori_loop(nblk // 2, nblk, attend, 0)
+    for side, o in ((0, 1), (1, -1)):
+        @pl.when(exists(o))
+        def _():
+            halo_copy(side).wait_recv()
+    for i, o in enumerate(OFFSETS):
+        @pl.when(exists(o))
+        def _():
+            far_copy(i).wait_recv()
+    for w, dst in ((wk, k), (wv, v)):
+        project(text, 0, BLK, w, dst, 0, BLK)
+        project(text, right0, BLK, w, dst, right0, BLK)
+        project(text, far0, NFAR * BLK, w, dst, far0, 128)
+
+    lax.fori_loop(nblk // 2, nblk, functools.partial(attend, True), 0)
 
     wait_bytes(ag2, ag2_r)
     for d in range(n):
@@ -310,7 +350,10 @@
         one = jnp.where(pos == grow_ref[...], 1.0, 0.0)
         is_g = jnp.max(one, axis=-1, keepdims=True) > 0.5
         put = jnp.dot(one.astype(BF), gq[...], preferred_element_type=F32)
-        att = jnp.where(is_g, put, sp[pl.ds(at, step)].astype(F32)).astype(BF)
+        own_rows = jnp.concatenate(
+            [sp[place[c * (step // BLK) + i]] for i in range(step // BLK)], axis=0
+        )
+        att = jnp.where(is_g, put, own_rows.astype(F32)).astype(BF)
         out_ref[pl.ds(at, step)] = jnp.dot(
             att, wo[...], preferred_element_type=F32
         ).astype(BF)
@@ -337,33 +380,23 @@
 def body(n, tokens, w_query, w_key, w_value, w_out, rand_blocks, global_pos):
     tok_dev, width = tokens.shape
     nblk = tok_dev // BLK
-    me = lax.axis_index("seq")
-    last = rand_blocks[:, RAND - 1]
-    owner = last // nblk
-    offs = jnp.array(OFFSETS, jnp.int32)
-    mine = owner[None, :] == (me + offs)[:, None]
-    want = jnp.sum(jnp.where(mine, (last - owner * nblk)[None, :], 0), axis=1)
-    req = jnp.broadcast_to(want[:, None, None], (NFAR, 8, 128)).astype(jnp.int32)
-    dist = rand_blocks // nblk - me
-    slot = jnp.where(dist < 0, dist + FAR, dist + FAR - 1)
-    idx = jnp.where(dist == 0, rand_blocks - me * nblk + 1, nblk + 2 + slot)
-    idx = idx.reshape(-1).astype(jnp.int32)
-
     cb = 256 if n <= 32 else 128
     rb = NG * width // (n * cb)
     ext = tok_dev + 2 * BLK + NFAR * BLK + NG
     dma = pltpu.SemaphoreType.DMA
     vm = pltpu.VMEM
     blocks = vm((ext // BLK, BLK, width), BF)
+    own_blocks = vm((nblk, BLK, width), BF)
     square = vm((width, width), BF)
     piece = vm((n, rb, cb), BF)
     stat = vm((n, rb, 128), F32)
     scratch = [
         vm((ext, width), BF), square, square, square, square,
-        vm((tok_dev, width), BF), blocks, blocks,
-        vm((NG, width), BF), vm((tok_dev, width), BF), vm((NG, width), F32),
+        own_blocks, blocks, blocks,
+        vm((NG, width), BF), own_blocks, vm((NG, width), F32),
         vm((NFAR * BLK, tok_dev), BF), vm((NFAR * BLK, width), BF),
-        vm((NFAR, 8, 128), jnp.int32),
+        vm((NFAR, 8, 128), F32), vm((NFAR, 8, 128), F32),
+        pltpu.SMEM((nblk,), jnp.int32), pltpu.SMEM((nblk,), jnp.int32),
         piece, piece, piece, piece, piece, stat, stat, piece,
         dma((5,)), dma((NFAR,)), dma((NFAR,)), dma((2 + NFAR,)), dma((2 + NFAR,)),
     ] + [dma(())] * 10
@@ -372,7 +405,7 @@
     return pl.pallas_call(
         functools.partial(mega, n),
         out_shape=jax.ShapeDtypeStruct((tok_dev, width), BF),
-        in_specs=[anyspace] * 5 + [vmem] * 3 + [pl.BlockSpec(memory_space=pltpu.SMEM)],
+        in_specs=[anyspace] * 5 + [vmem] * 2 + [pl.BlockSpec(memory_space=pltpu.SMEM)],
         out_specs=vmem,
         scratch_shapes=scratch,
         compiler_params=pltpu.CompilerParams(
@@ -380,8 +413,8 @@
         ),
         name="sublayer",
     )(
-        tokens, w_query, w_key, w_value, w_out, req,
-        global_pos.reshape(NG, 1), global_pos.reshape(1, NG), idx,
+        tokens, w_query, w_key, w_value, w_out, rand_blocks,
+        global_pos.reshape(1, NG), rand_blocks,
     )
 
 

time: 77.4 us -> 71.4 us (0.922)
  Pallas kernels: 69.1 us -> 66.6 us
  other arithmetic: 2.23 us -> 0 us
  local copies, waits for them, and re-layouts: 5.83 us -> 4.44 us
    pallas_call x1, Pallas kernels: 69.1 us -> 66.6 us  [body(): pl.pallas_call(functools.partial(mega, n), out_shape=jax.ShapeDtypeStruct...]
    reshape x2 -> x0, local copies, waits for them, and re-layouts: 2 us -> none  [the longest x1 1.39 us: body(): global_pos.reshape(NG, 1)]
    unnamed x1 -> x2, local copies, waits for them, and re-layouts: 3.08 us -> 4.44 us
where the time goes in v2:
time: 71.4 us; the launch traced here: 71.1 us
  Pallas kernels  66.6 us (93%)
  local copies, waits for them, and re-layouts  4.44 us (6%)
    pallas_call x1, Pallas kernels, body(): pl.pallas_call(functools.partial(mega, n), out_shape=jax.ShapeDtypeStruct...  66.6 us
    unnamed x2, local copies, waits for them, and re-layouts  4.44 us

profile of v2, /device:TPU:0, one launch (start us, length us, event | category | flops | bytes accessed | tf_op | source)
XLA Modules:
  0.0 71.1 jit_solution(14215160101973704175)
XLA Ops:
  0.0 1.4 %copy.8.rbv_ref.rb_ref = s32[16,3]{1,0:T(8,128)} copy(s32[16,3]{0,1:T(4,128)} %param.12) | data formatting | bytes 384 | tf_op args[5]
  1.4 66.6 %sublayer.1 = bf16[1024,1024]{1,0:T(8,128)(2,1)} custom-call(bf16[1024,1024]{1,0:T(8,128)(2,1)} %tok_hbm.1, bf16[1024,1024]{1,0:T(8,128)(2,1)} %wq_hbm.1, bf16[1024,1024]{1,0:T(8,128)(2,1)} %wk_hbm.1, bf16[1024,1024]{1,0:T(8,128)(2,1)} %wv_hbm.1, bf16[1024,1024]{1,0:T(8,128)(2,1)} %wo_hbm.1, s32[16,3]{1,0:T(8,128)} %copy.8.rbv_ref.rb_ref, s32[1,128]{1,0:T(1,128)} %bitcast.1, ...), custom_call_target="tpu_custom_call" | custom-call | tf_op jit(solution)/shard_map/sublayer/pallas_call | solution.py:405
  68.0 3.1 %copy.11 = bf16[1024,1024]{1,0:T(8,128)(2,1)} copy(bf16[1024,1024]{1,0:T(8,128)(2,1)} %sublayer.1) | data formatting | bytes 4194304
